TPU v7x, 256 devices: a whole 4x4x8 slice. The times are simulated.
256 devices in a mesh: node: 16 (over z, core), head: 16 (over x, y).
Axes of the slice: x: 4, y: 4, z: 8, core: 2. Of those that a mesh axis runs over, the one named last changes fastest.
Arguments:
- features: bfloat16 [65536, 1024], P(('node', 'head')), may hold values from -6 to 6
- attn_gain: float32 [1024], replicated, may hold values from 0.25 to 1.75
- qkv_weight: bfloat16 [1024, 16, 192], P(None, 'head')
- out_weight: bfloat16 [1024, 1024], replicated, may hold values from -0.1875 to 0.1875
- feedforward_norm_gain: float32 [1024], replicated, may hold values from 0.25 to 1.75
- up_weight: bfloat16 [1024, 2048], replicated, may hold values from -0.1875 to 0.1875
- down_weight: bfloat16 [2048, 1024], replicated, may hold values from -0.125 to 0.125
- tile_pattern: int32 [512, 8], P('node'), may hold values from 0 to 511, as said below
- node_order: int32 [16, 4096], P('node'), may hold values from 0 to 4095, each once within a row
Outputs:
- updated: bfloat16 [65536, 1024], P(('node', 'head'))
Inputs may be any that keep to these rules, and one draw needn't show every extreme that they name: `tile_pattern`: row t names 8 different tiles; the first is t itself; all lie in partitions (tiles p * 32 to (p + 1) * 32 - 1) at cyclic distance at most 2 from t's partition; the second lies 2 partitions below t's and the third 2 above. `node_order`: each row lists every local row of its partition once.
All inputs are finite; a program needn't handle non-finite values.
Results may differ from a plain program's by a relative error of at most 0.0045.
Values may be sent and summed in bfloat16 or wider, within the bound.
A program may use at most 64 MiB of HBM per device.

v0:
```python
import math
import jax
import jax.numpy as jnp
from jax import lax
from jax.sharding import PartitionSpec as P

D = 1024
HD = 64
TILE = 128
NNZ = 8
REACH = 2


def passed_along(x, axis, by):
    size = lax.axis_size(axis)
    return lax.ppermute(x, axis, [(i, (i + by) % size) for i in range(size)])


def layer_norm(values, gain):
    row_mean = jnp.mean(values, -1, keepdims=True)
    centred = values - row_mean
    variance = jnp.mean(centred * centred, -1, keepdims=True)
    return centred * lax.rsqrt(variance + 1e-05) * gain


def shards(
    features,
    attn_gain,
    qkv_weight,
    out_weight,
    feedforward_norm_gain,
    up_weight,
    down_weight,
    tile_pattern,
    node_order,
):
    own_rows = features.shape[0]
    local_heads = qkv_weight.shape[1]
    head_placements = lax.axis_size("head")
    partitions = lax.axis_size("node")
    rows_part = own_rows * head_placements
    query_tiles = rows_part // TILE
    normed = layer_norm(features.astype(jnp.float32), attn_gain).astype(jnp.bfloat16)
    reordered_weight = jnp.concatenate([qkv_weight[:, :, HD:], qkv_weight[:, :, :HD]], -1)
    local_weight = reordered_weight.reshape(D, local_heads * 3 * HD)
    projected = jnp.dot(
        lax.all_gather(normed, "head", axis=0, tiled=True),
        local_weight,
        preferred_element_type=jnp.float32,
    ).astype(jnp.bfloat16)
    projected = projected.reshape(rows_part, local_heads, 3 * HD)
    partition_permutation = node_order[0]
    keyval_rows = projected[:, :, : 2 * HD].reshape(rows_part, local_heads * 2 * HD)
    query_rows = projected[:, :, 2 * HD :].reshape(rows_part, local_heads * HD)
    keyval = jnp.take(keyval_rows, partition_permutation, axis=0)
    queries = jnp.take(query_rows, partition_permutation, axis=0)
    current = passed_along(keyval, "node", -REACH)
    blocks = [current]
    for cycle_step in range(2 * REACH):
        current = passed_along(current, "node", 1)
        blocks.append(current)
    window = jnp.stack(blocks[::-1])
    window_tiles = window.reshape((2 * REACH + 1) * query_tiles, TILE, local_heads * 2 * HD)
    partition = lax.axis_index("node")
    window_position = (
        tile_pattern // query_tiles - partition + REACH + partitions
    ) % partitions * query_tiles + tile_pattern % query_tiles
    tile_group = math.gcd(query_tiles, max(1, 512 // TILE))
    score_scale = 1.0 / math.sqrt(HD)

    def attend(item_pair):
        group_queries, columns = item_pair
        picked = jnp.take(window_tiles, columns.reshape(tile_group * NNZ), axis=0)
        picked = picked.reshape(tile_group, NNZ * TILE, local_heads, 2 * HD)
        key_rows = picked[..., :HD]
        value_rows = picked[..., HD:]
        query_block = group_queries.reshape(tile_group, TILE, local_heads, HD)
        scores = (
            jnp.einsum("gqhd,gmhd->ghqm", query_block, key_rows, preferred_element_type=jnp.float32)
            * score_scale
        )
        row_max = jnp.max(scores, -1, keepdims=True)
        expd = jnp.exp(scores - row_max)
        weight_arrays = (expd / jnp.sum(expd, -1, keepdims=True)).astype(jnp.bfloat16)
        result = jnp.einsum(
            "ghqm,gmhd->gqhd", weight_arrays, value_rows, preferred_element_type=jnp.float32
        ).astype(jnp.bfloat16)
        return result.reshape(tile_group * TILE, local_heads * HD)

    grouped_queries = queries.reshape(
        query_tiles // tile_group, tile_group * TILE, local_heads * HD
    )
    grouped_slots = window_position.reshape(query_tiles // tile_group, tile_group, NNZ)
    attended = lax.map(attend, (grouped_queries, grouped_slots)).reshape(
        rows_part, local_heads * HD
    )
    inverse_order = (
        jnp.zeros((rows_part,), jnp.int32)
        .at[partition_permutation]
        .set(jnp.arange(rows_part, dtype=jnp.int32))
    )
    restored = jnp.take(attended, inverse_order, axis=0)
    gathered_heads = lax.all_to_all(restored, "head", split_axis=0, concat_axis=1, tiled=True)
    residual = features.astype(jnp.float32) + jnp.dot(
        gathered_heads, out_weight, preferred_element_type=jnp.float32
    )
    mlp_input = layer_norm(residual, feedforward_norm_gain).astype(jnp.bfloat16)
    hidden = jax.nn.gelu(jnp.dot(mlp_input, up_weight, preferred_element_type=jnp.float32)).astype(
        jnp.bfloat16
    )
    return (residual + jnp.dot(hidden, down_weight, preferred_element_type=jnp.float32)).astype(
        jnp.bfloat16
    )


def solution(mesh):
    return jax.shard_map(
        shards,
        mesh=mesh,
        in_specs=(
            P(("node", "head"), None),
            P(),
            P(None, "head", None),
            P(),
            P(),
            P(),
            P(),
            P("node", None),
            P("node", None),
        ),
        out_specs=P(("node", "head"), None),
        check_vma=False,
    )
```

profile of v0, /device:TPU:96, one launch (start us, length us, event | category | flops | bytes accessed | tf_op | source)
XLA Modules:
  0.0 371.6 jit_solution(18285803736506806688)
XLA Ops:
  9.3 2.1 fusion.37
  11.5 77.8 %all-gather.2.cloned.1.call-done = bf16[4096,1024]{1,0:T(8,128)(2,1)} async-done(((bf16[256,1024]{1,0:T(8,128)(2,1)}), bf16[4096,1024]{1,0:T(8,128)(2,1)}) %all-gather.2.cloned.1.call-update) | async-done | bytes 8388624 | tf_op jit(solution)/shard_map/all_gather | solution.py:47
  89.3 6.3 %fusion.23 = bf16[4096,1,192]{0,2,1:T(8,128)(2,1)S(1)} fusion(bf16[4096,1024]{1,0:T(8,128)(2,1)} %all-gather.2.cloned.1.call-done, bf16[1024,1,64]{0,2,1:T(8,128)(2,1)S(1)} %slice-done, bf16[1024,1,128]{0,2,1:T(8,128)(2,1)S(1)} %slice-done.1), kind=kOutput, calls=%fused_computation.33 | convolution fusion | flops 1612185600 | bytes 10354688 | tf_op jit(solution)/shard_map/dot_general | solution.py:46
  99.4 15.0 %gather_fusion.1 = bf16[4096,128]{1,0:T(8,128)(2,1)} fusion(bf16[4096,128]{1,0:T(8,128)(2,1)S(1)} %copy.17, s32[4096]{0:T(1024)S(1)} %broadcast_clamp_fusion), kind=kCustom, calls=%fused_computation.3 | custom fusion | bytes 2113536 | tf_op jit(solution)/shard_map/jit(_take)/gather | solution.py:55
  114.4 3.4 broadcast_select_fusion.3
  118.3 25.5 %collective-permute-done = bf16[4096,128]{1,0:T(8,128)(2,1)S(1)} collective-permute-done((bf16[4096,128]{1,0:T(8,128)(2,1)S(1)}, bf16[4096,128]{1,0:T(8,128)(2,1)S(1)}, u32[]{:S(2)}, u32[]{:S(2)}) %collective-permute-start) | collective-permute-done | bytes 1048608 | tf_op jit(solution)/shard_map/ppermute | solution.py:16
  144.8 14.2 %collective-permute-done.1 = bf16[4096,128]{1,0:T(8,128)(2,1)S(1)} collective-permute-done((bf16[4096,128]{1,0:T(8,128)(2,1)S(1)}, bf16[4096,128]{1,0:T(8,128)(2,1)S(1)}, u32[]{:S(2)}, u32[]{:S(2)}) %collective-permute-start.1) | collective-permute-done | bytes 1048608 | tf_op jit(solution)/shard_map/ppermute | solution.py:16
  160.0 14.2 %collective-permute-done.2 = bf16[4096,128]{1,0:T(8,128)(2,1)S(1)} collective-permute-done((bf16[4096,128]{1,0:T(8,128)(2,1)S(1)}, bf16[4096,128]{1,0:T(8,128)(2,1)S(1)}, u32[]{:S(2)}, u32[]{:S(2)}) %collective-permute-start.2) | collective-permute-done | bytes 1048608 | tf_op jit(solution)/shard_map/ppermute | solution.py:16
  174.7 15.7 %scatter_custom_fusion = s32[4096]{0:T(1024)S(1)} fusion(s32[4096]{0:T(1024)S(1)} %bitcast.103, s32[4096]{0:T(1024)S(1)} %iota.3, s32[]{:T(128)} %copy.60), kind=kCustom, calls=%fused_computation.84 | custom fusion | bytes 16388 | tf_op jit(solution)/shard_map/scatter | solution.py:100
  190.5 3.7 collective-permute-start.4
  197.6 15.0 %gather_fusion.2 = bf16[4096,64]{1,0:T(8,128)(2,1)} fusion(bf16[4096,64]{1,0:T(8,128)(2,1)S(1)} %copy.18, s32[4096]{0:T(1024)S(1)} %get-tuple-element.53), kind=kCustom, calls=%fused_computation.clone | custom fusion | bytes 1064960 | tf_op jit(solution)/shard_map/jit(_take)/gather | solution.py:56
  212.6 3.4 broadcast_select_fusion.2
  221.4 2.3 copy-done.3
  223.7 92.5 %while.10 = (s32[]{:T(128)}, bf16[8,512,64]{1,2,0:T(8,128)(2,1)}, s32[8,4,8]{2,1,0:T(4,128)S(1)}, bf16[160,128,128]{2,1,0:T(8,128)(2,1)}, bf16[8,512,64]{1,2,0:T(8,128)(2,1)}, /*index=5*/s32[]{:T(128)}) while((s32[]{:T(128)}, bf16[8,512,64]{1,2,0:T(8,128)(2,1)}, s32[8,4,8]{2,1,0:T(4,128)S(1)}, bf16[160,128,128]{2,1,0:T(8,128)(2,1)}, ...), condition=%wide.region_5.7_spmd, body=%wide.region_2.6_spmd.sunk | while | flops 205557536 | bytes 12936373 | solution.py:94
  224.7 4.2 %gather_fusion = bf16[32,128,128]{2,1,0:T(8,128)(2,1)} fusion(bf16[160,128,128]{2,1,0:T(8,128)(2,1)} %get-tuple-element.105, s32[1024]{0:T(1024)S(1)} %pad_clamp_fusion.2), kind=kCustom, calls=%fused_computation.1.clone.1 | custom fusion | bytes 2097280 | tf_op jit(solution)/shard_map/while/body/eval_jaxpr/jit(_take)/gather | solution.py:73
  231.5 2.0 fusion.86
  236.3 4.2 %gather_fusion = bf16[32,128,128]{2,1,0:T(8,128)(2,1)} fusion(bf16[160,128,128]{2,1,0:T(8,128)(2,1)} %get-tuple-element.105, s32[1024]{0:T(1024)S(1)} %pad_clamp_fusion.2), kind=kCustom, calls=%fused_computation.1.clone.1 | custom fusion | bytes 2097280 | tf_op jit(solution)/shard_map/while/body/eval_jaxpr/jit(_take)/gather | solution.py:73
  243.1 2.0 fusion.86
  247.9 4.2 %gather_fusion = bf16[32,128,128]{2,1,0:T(8,128)(2,1)} fusion(bf16[160,128,128]{2,1,0:T(8,128)(2,1)} %get-tuple-element.105, s32[1024]{0:T(1024)S(1)} %pad_clamp_fusion.2), kind=kCustom, calls=%fused_computation.1.clone.1 | custom fusion | bytes 2097280 | tf_op jit(solution)/shard_map/while/body/eval_jaxpr/jit(_take)/gather | solution.py:73
  254.6 2.0 fusion.86
  259.4 4.2 %gather_fusion = bf16[32,128,128]{2,1,0:T(8,128)(2,1)} fusion(bf16[160,128,128]{2,1,0:T(8,128)(2,1)} %get-tuple-element.105, s32[1024]{0:T(1024)S(1)} %pad_clamp_fusion.2), kind=kCustom, calls=%fused_computation.1.clone.1 | custom fusion | bytes 2097280 | tf_op jit(solution)/shard_map/while/body/eval_jaxpr/jit(_take)/gather | solution.py:73
  266.2 2.0 fusion.86
  271.0 4.2 %gather_fusion = bf16[32,128,128]{2,1,0:T(8,128)(2,1)} fusion(bf16[160,128,128]{2,1,0:T(8,128)(2,1)} %get-tuple-element.105, s32[1024]{0:T(1024)S(1)} %pad_clamp_fusion.2), kind=kCustom, calls=%fused_computation.1.clone.1 | custom fusion | bytes 2097280 | tf_op jit(solution)/shard_map/while/body/eval_jaxpr/jit(_take)/gather | solution.py:73
  282.5 4.2 %gather_fusion = bf16[32,128,128]{2,1,0:T(8,128)(2,1)} fusion(bf16[160,128,128]{2,1,0:T(8,128)(2,1)} %get-tuple-element.105, s32[1024]{0:T(1024)S(1)} %pad_clamp_fusion.2), kind=kCustom, calls=%fused_computation.1.clone.1 | custom fusion | bytes 2097280 | tf_op jit(solution)/shard_map/while/body/eval_jaxpr/jit(_take)/gather | solution.py:73
  294.1 4.2 %gather_fusion = bf16[32,128,128]{2,1,0:T(8,128)(2,1)} fusion(bf16[160,128,128]{2,1,0:T(8,128)(2,1)} %get-tuple-element.105, s32[1024]{0:T(1024)S(1)} %pad_clamp_fusion.2), kind=kCustom, calls=%fused_computation.1.clone.1 | custom fusion | bytes 2097280 | tf_op jit(solution)/shard_map/while/body/eval_jaxpr/jit(_take)/gather | solution.py:73
  300.9 2.0 fusion.86
  305.7 4.2 %gather_fusion = bf16[32,128,128]{2,1,0:T(8,128)(2,1)} fusion(bf16[160,128,128]{2,1,0:T(8,128)(2,1)} %get-tuple-element.105, s32[1024]{0:T(1024)S(1)} %pad_clamp_fusion.2), kind=kCustom, calls=%fused_computation.1.clone.1 | custom fusion | bytes 2097280 | tf_op jit(solution)/shard_map/while/body/eval_jaxpr/jit(_take)/gather | solution.py:73
  312.4 2.0 fusion.86
  317.7 15.0 %gather_fusion.3 = bf16[4096,64]{1,0:T(8,128)(2,1)} fusion(bf16[4096,64]{1,0:T(8,128)(2,1)S(1)} %bitcast.94, s32[4096]{0:T(1024)S(1)} %get-tuple-element.54), kind=kCustom, calls=%fused_computation.2.clone | custom fusion | bytes 1064960 | tf_op jit(solution)/shard_map/jit(_take)/gather | solution.py:102
  332.7 4.3 %broadcast_select_fusion.1 = bf16[4096,64]{1,0:T(8,128)(2,1)} fusion(bf16[4096,64]{1,0:T(8,128)(2,1)} %gather_fusion.3, pred[4096]{0:T(1024)(128)(4,1)S(1)} %compare_and_fusion.1), kind=kLoop, calls=%fused_computation.65 | loop fusion | flops 262144 | bytes 1052672 | tf_op jit(solution)/shard_map/jit(_take)/select_n | solution.py:102
  338.5 16.7 %all_to_all.19 = bf16[16,256,64]{1,2,0:T(8,128)(2,1)S(1)} all-to-all(bf16[16,256,64]{1,2,0:T(8,128)(2,1)S(1)} %copy.21), channel_id=1, replica_groups=mesh['node'=16,'head'=16] {'head'}, dimensions={0} | all-to-all | bytes 1048576 | tf_op jit(solution)/shard_map/all_to_all | solution.py:103
  357.3 7.5 %fusion.32 = bf16[256,1024]{1,0:T(8,128)(2,1)} fusion(f32[256,1024]{1,0:T(8,128)} %copy-done.4, bf16[2048,1024]{1,0:T(8,128)(2,1)} %param.19, bf16[1024,2048]{1,0:T(8,128)(2,1)} %param.18, f32[1024]{0:T(1024)S(1)} %copy-done.14, f32[256]{0:T(256)S(1)} %add_rsqrt_fusion, f32[256]{0:T(256)S(1)} %broadcast_multiply_fusion), kind=kOutput, calls=%fused_computation.47 | convolution fusion | flops 2153775104 | bytes 9967616 | tf_op jit(solution)/shard_map/dot_general | solution.py:111
  (198 shorter events, 70.4 us)
Async XLA Ops:
  6.5 348.7 %copy-start = (bf16[1024,1024]{1,0:T(8,128)(2,1)S(1)}, bf16[1024,1024]{1,0:T(8,128)(2,1)}, u32[]{:S(2)}) copy-start(bf16[1024,1024]{1,0:T(8,128)(2,1)} %param.16) | copy-start | bytes 6291460
  6.5 82.7 %slice-start = ((bf16[1024,1,192]{0,2,1:T(8,128)(2,1)}), bf16[1024,1,64]{0,2,1:T(8,128)(2,1)S(1)}, s32[]{:S(2)}) async-start(bf16[1024,1,192]{0,2,1:T(8,128)(2,1)} %param.15), calls=%async_computation.2 | async-start | bytes 262144 | tf_op jit(solution)/shard_map/slice | solution.py:44
  6.5 82.7 %slice-start.1 = ((bf16[1024,1,192]{0,2,1:T(8,128)(2,1)}), bf16[1024,1,128]{0,2,1:T(8,128)(2,1)S(1)}, s32[]{:S(2)}) async-start(bf16[1024,1,192]{0,2,1:T(8,128)(2,1)} %param.15), calls=%async_computation.3 | async-start | bytes 524288 | tf_op jit(solution)/shard_map/slice | solution.py:44
  6.5 4.9 %copy-start.12 = (s32[1,4096]{1,0:T(1,128)S(1)}, s32[1,4096]{1,0:T(1,128)}, u32[]{:S(2)}) copy-start(s32[1,4096]{1,0:T(1,128)} %param.21) | copy-start | bytes 49156
  6.5 82.7 %all-gather.2.cloned.1.call-start = ((), (), s32[]{:S(2)}) async-start(), calls=%async_computation.1 | async-start | bytes 8912896 | tf_op jit(solution)/shard_map/all_gather | solution.py:47
  95.6 1.1 copy-start.5
  114.4 60.2 %copy-start.13 = (s32[32,8]{0,1:T(8,128)S(1)}, s32[32,8]{0,1:T(8,128)}, u32[]{:S(2)}) copy-start(s32[32,8]{0,1:T(8,128)} %param.20) | copy-start | bytes 3076
  117.8 26.0 %collective-permute-start = (bf16[4096,128]{1,0:T(8,128)(2,1)S(1)}, bf16[4096,128]{1,0:T(8,128)(2,1)S(1)}, u32[]{:S(2)}, u32[]{:S(2)}) collective-permute-start(bf16[4096,128]{1,0:T(8,128)(2,1)S(1)} %broadcast_select_fusion.3), channel_id=1, source_target_pairs={{0,224},{16,240},{32,0},{48,16},{64,32},{80,48},{96,64},{112,80},{... | collective-permute-start | bytes 3145736 | tf_op jit(solution)/shard_map/ppermute | solution.py:16
  143.8 1.0 copy-start.6
  144.8 14.2 %collective-permute-start.1 = (bf16[4096,128]{1,0:T(8,128)(2,1)S(1)}, bf16[4096,128]{1,0:T(8,128)(2,1)S(1)}, u32[]{:S(2)}, u32[]{:S(2)}) collective-permute-start(bf16[4096,128]{1,0:T(8,128)(2,1)S(1)} %collective-permute-done), channel_id=1, source_target_pairs={{0,16},{16,32},{32,48},{48,64},{64,80},{80,96},{96,112},{112,128},... | collective-permute-start | bytes 3145736 | tf_op jit(solution)/shard_map/ppermute | solution.py:16
  159.0 1.0 copy-start.8
  160.0 14.2 %collective-permute-start.2 = (bf16[4096,128]{1,0:T(8,128)(2,1)S(1)}, bf16[4096,128]{1,0:T(8,128)(2,1)S(1)}, u32[]{:S(2)}, u32[]{:S(2)}) collective-permute-start(bf16[4096,128]{1,0:T(8,128)(2,1)S(1)} %collective-permute-done.1), channel_id=1, source_target_pairs={{0,16},{16,32},{32,48},{48,64},{64,80},{80,96},{96,112},{112,128},... | collective-permute-start | bytes 3145736 | tf_op jit(solution)/shard_map/ppermute | solution.py:16
  174.2 20.0 %copy-start.10 = (bf16[4096,128]{1,0:T(8,128)(2,1)}, bf16[4096,128]{1,0:T(8,128)(2,1)S(1)}, u32[]{:S(2)}) copy-start(bf16[4096,128]{1,0:T(8,128)(2,1)S(1)} %collective-permute-done.2) | copy-start | bytes 3145732
  174.2 16.3 %collective-permute-start.3 = (bf16[4096,128]{1,0:T(8,128)(2,1)S(1)}, bf16[4096,128]{1,0:T(8,128)(2,1)}, u32[]{:S(2)}, u32[]{:S(2)}) collective-permute-start(bf16[4096,128]{1,0:T(8,128)(2,1)S(1)} %collective-permute-done.2), channel_id=1, source_target_pairs={{0,16},{16,32},{32,48},{48,64},{64,80},{80,96},{96,112},{112,128},... | collective-permute-start | bytes 3145736 | tf_op jit(solution)/shard_map/ppermute | solution.py:16
  190.5 26.6 %collective-permute-start.4 = (bf16[4096,128]{1,0:T(8,128)(2,1)}, bf16[4096,128]{1,0:T(8,128)(2,1)}, u32[]{:S(2)}, u32[]{:S(2)}) collective-permute-start(bf16[4096,128]{1,0:T(8,128)(2,1)} %collective-permute-done.3), channel_id=1, source_target_pairs={{0,16},{16,32},{32,48},{48,64},{64,80},{80,96},{96,112},{112,128},... | collective-permute-start | bytes 3145736 | tf_op jit(solution)/shard_map/ppermute | solution.py:16
  217.1 2.9 copy-start.11
  218.5 1.6 copy-start.9
  220.0 1.3 copy-start.7
  221.4 2.3 copy-start.3
  231.5 2.0 copy-start.1
  243.1 2.0 copy-start.1
  254.6 2.0 copy-start.1
  266.2 2.0 copy-start.1
  277.8 2.0 copy-start.1
  289.3 2.0 copy-start.1
  300.9 2.0 copy-start.1
  312.4 2.0 copy-start.1
  332.7 22.6 %copy-start.2 = (bf16[256,1024]{1,0:T(8,128)(2,1)S(1)}, bf16[256,1024]{1,0:T(8,128)(2,1)}, u32[]{:S(2)}) copy-start(bf16[256,1024]{1,0:T(8,128)(2,1)} %param.13) | copy-start | bytes 1572868
  355.2 2.1 copy-start.14
  356.1 1.0 copy-start.4
Sparse Core Ops, SparseCore 0:
  11.6 77.6 all-gather.1
where the time goes:
time: 373 us; the launch traced here: 372 us
  local copies, waits for them, and re-layouts  141 us (38%)
  waiting for transfers between devices  132 us (35%)
  matrix products  38.1 us (10%)
  other arithmetic  25.3 us (7%)
  blocking collectives  16.7 us (4%)
  between operations  13.6 us (4%)
  starting transfers between devices  4.69 us (1%)
    all_gather x1, waiting for transfers between devices, shards(): lax.all_gather(normed, 'head', axis=0, tiled=True)  77.8 us
    ppermute x5, waiting for transfers between devices, passed_along(): return lax.ppermute(x, axis, [(i, (i + by) % size) for i in range(size)])  53.9 us
    gather x16, local copies, waits for them, and re-layouts, attend(): picked = jnp.take(window_tiles, columns.reshape(tile_group * NNZ), axis=0)  45.3 us
    all_to_all x1, blocking collectives, shards(): lax.all_to_all(restored, 'head', split_axis=0, concat_axis=1, tiled=True)  16.7 us
    sub x8, matrix products, attend(): expd = jnp.exp(scores - row_max)  15.7 us
    scatter x1, local copies, waits for them, and re-layouts, shards(): inverse_order = jnp.zeros((rows_part,), jnp.int32).at[partition_permutati...  15.7 us
    gather x1, local copies, waits for them, and re-layouts, shards(): keyval = jnp.take(keyval_rows, partition_permutation, axis=0)  15 us
    gather x1, local copies, waits for them, and re-layouts, shards(): restored = jnp.take(attended, inverse_order, axis=0)  15 us
  transfers between devices with their start and end apart: 6, of which 4 were waited for; matrix products, arithmetic and copies ran while one was open for 10% of the time, Pallas kernels for 0%

commit v1 on v0

--- a/solution.py
+++ b/solution.py
@@ -100,7 +100,10 @@
         .set(jnp.arange(rows_part, dtype=jnp.int32))
     )
     restored = jnp.take(attended, inverse_order, axis=0)
-    gathered_heads = lax.all_to_all(restored, "head", split_axis=0, concat_axis=1, tiled=True)
+    gathered_heads = jnp.concatenate(
+        lax.all_to_all(jnp.stack(jnp.split(restored, lax.axis_size("head"), axis=0)), "head", 0, 0),
+        axis=1,
+    )
     residual = features.astype(jnp.float32) + jnp.dot(
         gathered_heads, out_weight, preferred_element_type=jnp.float32
     )

time: 373 us -> 383 us (1.027)
  local copies, waits for them, and re-layouts: 141 us -> 151 us
    unnamed x32 -> x47, local copies, waits for them, and re-layouts: 10.4 us -> 19.9 us
where the time goes in v1:
time: 383 us; the launch traced here: 381 us
  local copies, waits for them, and re-layouts  151 us (39%)
  waiting for transfers between devices  132 us (34%)
  matrix products  38.1 us (10%)
  other arithmetic  24.4 us (6%)
  blocking collectives  16.7 us (4%)
  between operations  13.7 us (4%)
  starting transfers between devices  4.69 us (1%)
    all_gather x1, waiting for transfers between devices, shards(): lax.all_gather(normed, 'head', axis=0, tiled=True)  77.8 us
    ppermute x5, waiting for transfers between devices, passed_along(): return lax.ppermute(x, axis, [(i, (i + by) % size) for i in range(size)])  53.9 us
    gather x16, local copies, waits for them, and re-layouts, attend(): picked = jnp.take(window_tiles, columns.reshape(tile_group * NNZ), axis=0)  45.3 us
    unnamed x47, local copies, waits for them, and re-layouts  19.9 us
    all_to_all x1, blocking collectives, shards(): lax.all_to_all(jnp.stack(jnp.split(restored, lax.axis_size('head'), axis=...  16.7 us
    sub x8, matrix products, attend(): expd = jnp.exp(scores - row_max)  15.7 us
    scatter x1, local copies, waits for them, and re-layouts, shards(): inverse_order = jnp.zeros((rows_part,), jnp.int32).at[partition_permutati...  15.7 us
    gather x1, local copies, waits for them, and re-layouts, shards(): keyval = jnp.take(keyval_rows, partition_permutation, axis=0)  15 us
  transfers between devices with their start and end apart: 6, of which 4 were waited for; matrix products, arithmetic and copies ran while one was open for 10% of the time, Pallas kernels for 0%

profile of v1, /device:TPU:96, one launch (start us, length us, event | category | flops | bytes accessed | tf_op | source)
XLA Modules:
  0.0 380.8 jit_solution(12906450693837003388)
XLA Ops:
  9.3 2.1 fusion.37
  11.5 77.8 %all-gather.2.cloned.1.call-done = bf16[4096,1024]{1,0:T(8,128)(2,1)} async-done(((bf16[256,1024]{1,0:T(8,128)(2,1)}), bf16[4096,1024]{1,0:T(8,128)(2,1)}) %all-gather.2.cloned.1.call-update) | async-done | bytes 8388624 | tf_op jit(solution)/shard_map/all_gather | solution.py:47
  89.3 6.3 %fusion.23 = bf16[4096,1,192]{0,2,1:T(8,128)(2,1)S(1)} fusion(bf16[4096,1024]{1,0:T(8,128)(2,1)} %all-gather.2.cloned.1.call-done, bf16[1024,1,64]{0,2,1:T(8,128)(2,1)S(1)} %slice-done, bf16[1024,1,128]{0,2,1:T(8,128)(2,1)S(1)} %slice-done.1), kind=kOutput, calls=%fused_computation.33 | convolution fusion | flops 1612185600 | bytes 10354688 | tf_op jit(solution)/shard_map/dot_general | solution.py:46
  99.4 15.0 %gather_fusion.1 = bf16[4096,128]{1,0:T(8,128)(2,1)} fusion(bf16[4096,128]{1,0:T(8,128)(2,1)S(1)} %copy.26, s32[4096]{0:T(1024)S(1)} %broadcast_clamp_fusion), kind=kCustom, calls=%fused_computation.3 | custom fusion | bytes 2113536 | tf_op jit(solution)/shard_map/jit(_take)/gather | solution.py:55
  114.4 3.4 broadcast_select_fusion.3
  118.3 25.5 %collective-permute-done = bf16[4096,128]{1,0:T(8,128)(2,1)S(1)} collective-permute-done((bf16[4096,128]{1,0:T(8,128)(2,1)S(1)}, bf16[4096,128]{1,0:T(8,128)(2,1)S(1)}, u32[]{:S(2)}, u32[]{:S(2)}) %collective-permute-start) | collective-permute-done | bytes 1048608 | tf_op jit(solution)/shard_map/ppermute | solution.py:16
  144.8 14.2 %collective-permute-done.1 = bf16[4096,128]{1,0:T(8,128)(2,1)S(1)} collective-permute-done((bf16[4096,128]{1,0:T(8,128)(2,1)S(1)}, bf16[4096,128]{1,0:T(8,128)(2,1)S(1)}, u32[]{:S(2)}, u32[]{:S(2)}) %collective-permute-start.1) | collective-permute-done | bytes 1048608 | tf_op jit(solution)/shard_map/ppermute | solution.py:16
  160.0 14.2 %collective-permute-done.2 = bf16[4096,128]{1,0:T(8,128)(2,1)S(1)} collective-permute-done((bf16[4096,128]{1,0:T(8,128)(2,1)S(1)}, bf16[4096,128]{1,0:T(8,128)(2,1)S(1)}, u32[]{:S(2)}, u32[]{:S(2)}) %collective-permute-start.2) | collective-permute-done | bytes 1048608 | tf_op jit(solution)/shard_map/ppermute | solution.py:16
  174.7 15.7 %scatter_custom_fusion = s32[4096]{0:T(1024)S(1)} fusion(s32[4096]{0:T(1024)S(1)} %bitcast.165, s32[4096]{0:T(1024)S(1)} %iota.3, s32[]{:T(128)} %copy.84), kind=kCustom, calls=%fused_computation.116 | custom fusion | bytes 16388 | tf_op jit(solution)/shard_map/scatter | solution.py:100
  190.5 3.7 collective-permute-start.4
  197.6 15.0 %gather_fusion.2 = bf16[4096,64]{1,0:T(8,128)(2,1)} fusion(bf16[4096,64]{1,0:T(8,128)(2,1)S(1)} %copy.27, s32[4096]{0:T(1024)S(1)} %get-tuple-element.58), kind=kCustom, calls=%fused_computation.clone | custom fusion | bytes 1064960 | tf_op jit(solution)/shard_map/jit(_take)/gather | solution.py:56
  212.6 3.4 broadcast_select_fusion.2
  221.4 2.3 copy-done.3
  223.7 92.5 %while.10 = (s32[]{:T(128)}, bf16[8,512,64]{1,2,0:T(8,128)(2,1)}, s32[8,4,8]{2,1,0:T(4,128)S(1)}, bf16[160,128,128]{2,1,0:T(8,128)(2,1)}, bf16[8,512,64]{1,2,0:T(8,128)(2,1)}, /*index=5*/s32[]{:T(128)}) while((s32[]{:T(128)}, bf16[8,512,64]{1,2,0:T(8,128)(2,1)}, s32[8,4,8]{2,1,0:T(4,128)S(1)}, bf16[160,128,128]{2,1,0:T(8,128)(2,1)}, ...), condition=%wide.region_5.7_spmd, body=%wide.region_2.6_spmd.sunk | while | flops 205557536 | bytes 12936373 | solution.py:94
  224.7 4.2 %gather_fusion = bf16[32,128,128]{2,1,0:T(8,128)(2,1)} fusion(bf16[160,128,128]{2,1,0:T(8,128)(2,1)} %get-tuple-element.110, s32[1024]{0:T(1024)S(1)} %pad_clamp_fusion.2), kind=kCustom, calls=%fused_computation.1.clone.1 | custom fusion | bytes 2097280 | tf_op jit(solution)/shard_map/while/body/eval_jaxpr/jit(_take)/gather | solution.py:73
  231.5 2.0 fusion.102
  236.3 4.2 %gather_fusion = bf16[32,128,128]{2,1,0:T(8,128)(2,1)} fusion(bf16[160,128,128]{2,1,0:T(8,128)(2,1)} %get-tuple-element.110, s32[1024]{0:T(1024)S(1)} %pad_clamp_fusion.2), kind=kCustom, calls=%fused_computation.1.clone.1 | custom fusion | bytes 2097280 | tf_op jit(solution)/shard_map/while/body/eval_jaxpr/jit(_take)/gather | solution.py:73
  243.1 2.0 fusion.102
  247.9 4.2 %gather_fusion = bf16[32,128,128]{2,1,0:T(8,128)(2,1)} fusion(bf16[160,128,128]{2,1,0:T(8,128)(2,1)} %get-tuple-element.110, s32[1024]{0:T(1024)S(1)} %pad_clamp_fusion.2), kind=kCustom, calls=%fused_computation.1.clone.1 | custom fusion | bytes 2097280 | tf_op jit(solution)/shard_map/while/body/eval_jaxpr/jit(_take)/gather | solution.py:73
  254.6 2.0 fusion.102
  259.4 4.2 %gather_fusion = bf16[32,128,128]{2,1,0:T(8,128)(2,1)} fusion(bf16[160,128,128]{2,1,0:T(8,128)(2,1)} %get-tuple-element.110, s32[1024]{0:T(1024)S(1)} %pad_clamp_fusion.2), kind=kCustom, calls=%fused_computation.1.clone.1 | custom fusion | bytes 2097280 | tf_op jit(solution)/shard_map/while/body/eval_jaxpr/jit(_take)/gather | solution.py:73
  266.2 2.0 fusion.102
  271.0 4.2 %gather_fusion = bf16[32,128,128]{2,1,0:T(8,128)(2,1)} fusion(bf16[160,128,128]{2,1,0:T(8,128)(2,1)} %get-tuple-element.110, s32[1024]{0:T(1024)S(1)} %pad_clamp_fusion.2), kind=kCustom, calls=%fused_computation.1.clone.1 | custom fusion | bytes 2097280 | tf_op jit(solution)/shard_map/while/body/eval_jaxpr/jit(_take)/gather | solution.py:73
  282.5 4.2 %gather_fusion = bf16[32,128,128]{2,1,0:T(8,128)(2,1)} fusion(bf16[160,128,128]{2,1,0:T(8,128)(2,1)} %get-tuple-element.110, s32[1024]{0:T(1024)S(1)} %pad_clamp_fusion.2), kind=kCustom, calls=%fused_computation.1.clone.1 | custom fusion | bytes 2097280 | tf_op jit(solution)/shard_map/while/body/eval_jaxpr/jit(_take)/gather | solution.py:73
  294.1 4.2 %gather_fusion = bf16[32,128,128]{2,1,0:T(8,128)(2,1)} fusion(bf16[160,128,128]{2,1,0:T(8,128)(2,1)} %get-tuple-element.110, s32[1024]{0:T(1024)S(1)} %pad_clamp_fusion.2), kind=kCustom, calls=%fused_computation.1.clone.1 | custom fusion | bytes 2097280 | tf_op jit(solution)/shard_map/while/body/eval_jaxpr/jit(_take)/gather | solution.py:73
  300.9 2.0 fusion.102
  305.7 4.2 %gather_fusion = bf16[32,128,128]{2,1,0:T(8,128)(2,1)} fusion(bf16[160,128,128]{2,1,0:T(8,128)(2,1)} %get-tuple-element.110, s32[1024]{0:T(1024)S(1)} %pad_clamp_fusion.2), kind=kCustom, calls=%fused_computation.1.clone.1 | custom fusion | bytes 2097280 | tf_op jit(solution)/shard_map/while/body/eval_jaxpr/jit(_take)/gather | solution.py:73
  312.4 2.0 fusion.102
  317.7 15.0 %gather_fusion.3 = bf16[4096,64]{1,0:T(8,128)(2,1)} fusion(bf16[4096,64]{1,0:T(8,128)(2,1)S(1)} %bitcast.157, s32[4096]{0:T(1024)S(1)} %get-tuple-element.59), kind=kCustom, calls=%fused_computation.2.clone | custom fusion | bytes 1064960 | tf_op jit(solution)/shard_map/jit(_take)/gather | solution.py:102
  332.7 3.4 broadcast_select_fusion.1
  347.7 16.7 %all_to_all.5 = bf16[16,256,64]{1,2,0:T(8,128)(2,1)S(1)} all-to-all(bf16[16,256,64]{1,2,0:T(8,128)(2,1)S(1)} %copy.30), channel_id=1, replica_groups=mesh['node'=16,'head'=16] {'head'}, dimensions={0} | all-to-all | bytes 1048576 | tf_op jit(solution)/shard_map/all_to_all | solution.py:104
  366.5 7.5 %fusion.32 = bf16[256,1024]{1,0:T(8,128)(2,1)} fusion(f32[256,1024]{1,0:T(8,128)} %copy-done.4, bf16[2048,1024]{1,0:T(8,128)(2,1)} %param.19, bf16[1024,2048]{1,0:T(8,128)(2,1)} %param.18, f32[1024]{0:T(1024)S(1)} %copy-done.14, f32[256]{0:T(256)S(1)} %add_rsqrt_fusion, f32[256]{0:T(256)S(1)} %broadcast_multiply_fusion), kind=kOutput, calls=%fused_computation.47 | convolution fusion | flops 2153775104 | bytes 9967616 | tf_op jit(solution)/shard_map/dot_general | solution.py:114
  (214 shorter events, 80.5 us)
Async XLA Ops:
  6.5 357.9 %copy-start = (bf16[1024,1024]{1,0:T(8,128)(2,1)S(1)}, bf16[1024,1024]{1,0:T(8,128)(2,1)}, u32[]{:S(2)}) copy-start(bf16[1024,1024]{1,0:T(8,128)(2,1)} %param.16) | copy-start | bytes 6291460
  6.5 82.7 %slice-start = ((bf16[1024,1,192]{0,2,1:T(8,128)(2,1)}), bf16[1024,1,64]{0,2,1:T(8,128)(2,1)S(1)}, s32[]{:S(2)}) async-start(bf16[1024,1,192]{0,2,1:T(8,128)(2,1)} %param.15), calls=%async_computation.2 | async-start | bytes 262144 | tf_op jit(solution)/shard_map/slice | solution.py:44
  6.5 82.7 %slice-start.1 = ((bf16[1024,1,192]{0,2,1:T(8,128)(2,1)}), bf16[1024,1,128]{0,2,1:T(8,128)(2,1)S(1)}, s32[]{:S(2)}) async-start(bf16[1024,1,192]{0,2,1:T(8,128)(2,1)} %param.15), calls=%async_computation.3 | async-start | bytes 524288 | tf_op jit(solution)/shard_map/slice | solution.py:44
  6.5 4.9 %copy-start.12 = (s32[1,4096]{1,0:T(1,128)S(1)}, s32[1,4096]{1,0:T(1,128)}, u32[]{:S(2)}) copy-start(s32[1,4096]{1,0:T(1,128)} %param.21) | copy-start | bytes 49156
  6.5 82.7 %all-gather.2.cloned.1.call-start = ((), (), s32[]{:S(2)}) async-start(), calls=%async_computation.1 | async-start | bytes 8912896 | tf_op jit(solution)/shard_map/all_gather | solution.py:47
  95.6 1.1 copy-start.5
  114.4 60.2 %copy-start.13 = (s32[32,8]{0,1:T(8,128)S(1)}, s32[32,8]{0,1:T(8,128)}, u32[]{:S(2)}) copy-start(s32[32,8]{0,1:T(8,128)} %param.20) | copy-start | bytes 3076
  117.8 26.0 %collective-permute-start = (bf16[4096,128]{1,0:T(8,128)(2,1)S(1)}, bf16[4096,128]{1,0:T(8,128)(2,1)S(1)}, u32[]{:S(2)}, u32[]{:S(2)}) collective-permute-start(bf16[4096,128]{1,0:T(8,128)(2,1)S(1)} %broadcast_select_fusion.3), channel_id=1, source_target_pairs={{0,224},{16,240},{32,0},{48,16},{64,32},{80,48},{96,64},{112,80},{... | collective-permute-start | bytes 3145736 | tf_op jit(solution)/shard_map/ppermute | solution.py:16
  143.8 1.0 copy-start.6
  144.8 14.2 %collective-permute-start.1 = (bf16[4096,128]{1,0:T(8,128)(2,1)S(1)}, bf16[4096,128]{1,0:T(8,128)(2,1)S(1)}, u32[]{:S(2)}, u32[]{:S(2)}) collective-permute-start(bf16[4096,128]{1,0:T(8,128)(2,1)S(1)} %collective-permute-done), channel_id=1, source_target_pairs={{0,16},{16,32},{32,48},{48,64},{64,80},{80,96},{96,112},{112,128},... | collective-permute-start | bytes 3145736 | tf_op jit(solution)/shard_map/ppermute | solution.py:16
  159.0 1.0 copy-start.8
  160.0 14.2 %collective-permute-start.2 = (bf16[4096,128]{1,0:T(8,128)(2,1)S(1)}, bf16[4096,128]{1,0:T(8,128)(2,1)S(1)}, u32[]{:S(2)}, u32[]{:S(2)}) collective-permute-start(bf16[4096,128]{1,0:T(8,128)(2,1)S(1)} %collective-permute-done.1), channel_id=1, source_target_pairs={{0,16},{16,32},{32,48},{48,64},{64,80},{80,96},{96,112},{112,128},... | collective-permute-start | bytes 3145736 | tf_op jit(solution)/shard_map/ppermute | solution.py:16
  174.2 20.0 %copy-start.10 = (bf16[4096,128]{1,0:T(8,128)(2,1)}, bf16[4096,128]{1,0:T(8,128)(2,1)S(1)}, u32[]{:S(2)}) copy-start(bf16[4096,128]{1,0:T(8,128)(2,1)S(1)} %collective-permute-done.2) | copy-start | bytes 3145732
  174.2 16.3 %collective-permute-start.3 = (bf16[4096,128]{1,0:T(8,128)(2,1)S(1)}, bf16[4096,128]{1,0:T(8,128)(2,1)}, u32[]{:S(2)}, u32[]{:S(2)}) collective-permute-start(bf16[4096,128]{1,0:T(8,128)(2,1)S(1)} %collective-permute-done.2), channel_id=1, source_target_pairs={{0,16},{16,32},{32,48},{48,64},{64,80},{80,96},{96,112},{112,128},... | collective-permute-start | bytes 3145736 | tf_op jit(solution)/shard_map/ppermute | solution.py:16
  190.5 26.6 %collective-permute-start.4 = (bf16[4096,128]{1,0:T(8,128)(2,1)}, bf16[4096,128]{1,0:T(8,128)(2,1)}, u32[]{:S(2)}, u32[]{:S(2)}) collective-permute-start(bf16[4096,128]{1,0:T(8,128)(2,1)} %collective-permute-done.3), channel_id=1, source_target_pairs={{0,16},{16,32},{32,48},{48,64},{64,80},{80,96},{96,112},{112,128},... | collective-permute-start | bytes 3145736 | tf_op jit(solution)/shard_map/ppermute | solution.py:16
  217.1 2.9 copy-start.11
  218.5 1.6 copy-start.9
  220.0 1.3 copy-start.7
  221.4 2.3 copy-start.3
  231.5 2.0 copy-start.1
  243.1 2.0 copy-start.1
  254.6 2.0 copy-start.1
  266.2 2.0 copy-start.1
  277.8 2.0 copy-start.1
  289.3 2.0 copy-start.1
  300.9 2.0 copy-start.1
  312.4 2.0 copy-start.1
  338.6 25.9 %copy-start.2 = (bf16[256,1024]{1,0:T(8,128)(2,1)S(1)}, bf16[256,1024]{1,0:T(8,128)(2,1)}, u32[]{:S(2)}) copy-start(bf16[256,1024]{1,0:T(8,128)(2,1)} %param.13) | copy-start | bytes 1572868
  364.5 2.1 copy-start.14
  365.3 1.0 copy-start.4
Sparse Core Ops, SparseCore 0:
  11.6 77.6 all-gather.1
